TPU v7x, 256 devices: a whole 4x4x8 slice. The times are simulated.
256 devices in a mesh: ctx: 128 (over z, x_lo, y, core), head: 2 (over x_hi).
Axes of the slice: x: 4 (x_hi: 2, x_lo: 2; x = x_hi * 2 + x_lo), y: 4, z: 8, core: 2. Of those that a mesh axis runs over, the one named last changes fastest.
Arguments:
- queries: bfloat16 [65536, 2048], P('ctx', 'head'), may hold values from -13 to 13, as said below
- keys: bfloat16 [65536, 512], P('ctx', 'head'), may hold values from -13 to 13
- values: bfloat16 [65536, 512], P('ctx', 'head'), may hold values from -24 to 24
- positions: int32 [65536], P('ctx'), may hold values from 0 to 32767, as said below
- out_weight: bfloat16 [2048, 4096], P(None, 'head'), may hold values from -0.125 to 0.125
Outputs:
- mixed: bfloat16 [65536, 4096], P('ctx', 'head')
Inputs may be any that keep to these rules, and one draw needn't show every extreme that they name: queries, keys: every entry lies in the stated range. positions[r] is 0 where the token at sequence position g(r) begins a document and one more than the position of the token at g(r) - 1 otherwise; documents begin at sequence positions 0 and 32768 and possibly elsewhere in the first half; the second half is one document.
All inputs are finite; a program needn't handle non-finite values.
Results may differ from a plain program's by a relative error of at most 0.012.
The roundings to bfloat16 on the way count: a program that leaves them out, or rounds other values in their place, can miss the bound.
Values may be sent and summed in bfloat16 or wider, within the bound.
A program may use at most 128 MiB of HBM per device.

v0:
```python
import math
import jax
import jax.numpy as jnp
import numpy as np
from jax import lax
from jax.sharding import PartitionSpec as P

HEAD_SIZE = 128
STEPS = 4
neg_large = -1e30


def passed_along(value, axis, steps):
    count = lax.axis_size(axis)
    pairs = [(source, (source + steps) % count) for source in range(count)]
    return lax.ppermute(value, axis, pairs)


def rotate(block, positions, width):
    halfway = width // 2
    table = np.power(500000.0, -2.0 * np.arange(halfway) / width).astype(np.float32)
    angle = positions.astype(jnp.float32)[:, None] * jnp.asarray(table, dtype=jnp.float32)[None, :]
    cosine = jnp.cos(angle)[:, None, :]
    sinus = jnp.sin(angle)[:, None, :]
    number = block.shape[0]
    groups = block.shape[1] // width
    split_up = block.astype(jnp.float32).reshape(number, groups, width)
    leading = split_up[:, :, :halfway]
    trailing = split_up[:, :, halfway:]
    turned = jnp.concatenate(
        [leading * cosine - trailing * sinus, trailing * cosine + leading * sinus], axis=2
    )
    return turned.reshape(number, groups * width).astype(jnp.bfloat16)


def make_index(block_number, cycle_size, number):
    halfway = number // 2
    within = jnp.arange(number, dtype=jnp.int32)
    early = block_number * halfway + within
    late = (2 * cycle_size - 1 - block_number) * halfway + within - halfway
    return jnp.where(within < halfway, early, late)


def attend(
    state, query_part, query_index, query_start, key_part, value_part, key_index, query_group
):
    maxima, totals, sums = state
    number = query_part.shape[0]
    shaped_query = query_part.reshape(number, -1, query_group, HEAD_SIZE)
    shaped_key = key_part.reshape(key_part.shape[0], -1, HEAD_SIZE)
    shaped_value = value_part.reshape(value_part.shape[0], -1, HEAD_SIZE)
    scores = jnp.einsum(
        "qhgd,khd->hgqk", shaped_query, shaped_key, preferred_element_type=jnp.float32
    ) * (1.0 / math.sqrt(HEAD_SIZE))
    allowed = (key_index[None, :] <= query_index[:, None]) & (
        key_index[None, :] >= query_start[:, None]
    )
    scores = jnp.where(allowed, scores, neg_large)
    updated = jnp.maximum(maxima, jnp.max(scores, axis=3))
    weights = jnp.where(allowed, jnp.exp(scores - updated[..., None]), 0.0)
    factor = jnp.exp(maxima - updated)
    totals = totals * factor + jnp.sum(weights, axis=3)
    added = jnp.einsum(
        "hgqk,khd->qhgd",
        weights.astype(jnp.bfloat16),
        shaped_value,
        preferred_element_type=jnp.float32,
    )
    sums = sums * jnp.transpose(factor, (2, 0, 1))[..., None] + added
    return (updated, totals, sums)


def attend_rows(
    state, lower, upper, q_rot, index_of, doc_start, key_part, value_part, key_index, query_group
):
    maxima, totals, sums = state
    sliced = (maxima, totals, sums)
    new_max, new_total, new_sums = attend(
        sliced, q_rot, index_of, doc_start, key_part, value_part, key_index, query_group
    )
    return (
        maxima.at[:, :, lower:upper].set(new_max),
        totals.at[:, :, lower:upper].set(new_total),
        sums.at[lower:upper].set(new_sums),
    )


def shards(queries, keys, values, positions, out_weight):
    number = queries.shape[0]
    cycle_size = lax.axis_size("ctx")
    rank = lax.axis_index("ctx")
    kv_local = keys.shape[1] // HEAD_SIZE
    query_group = queries.shape[1] // keys.shape[1]
    index_of = make_index(rank, cycle_size, number)
    doc_start = index_of - positions
    q_rot = rotate(queries, positions, HEAD_SIZE)
    rotary_keys = rotate(keys, positions, HEAD_SIZE)
    state = (
        jnp.full((kv_local, query_group, number), neg_large, jnp.float32),
        jnp.zeros((kv_local, query_group, number), jnp.float32),
        jnp.zeros((number, kv_local, query_group, HEAD_SIZE), jnp.float32),
    )
    state = attend_rows(
        state, 0, number, q_rot, index_of, doc_start, rotary_keys, values, index_of, query_group
    )
    travel = (rotary_keys, values)
    for step in range(1, STEPS):
        travel = passed_along((travel[0], travel[1]), "ctx", 1)
        key_row_slice, value_rows = travel
        source = (rank - step) % cycle_size
        key_index = make_index(source, cycle_size, number)
        state = attend_rows(
            state,
            0,
            number,
            q_rot,
            index_of,
            doc_start,
            key_row_slice,
            value_rows,
            key_index,
            query_group,
        )
    maxima, totals, sums = state
    attended = (
        (sums / jnp.transpose(totals, (2, 0, 1))[..., None])
        .reshape(number, kv_local * query_group * HEAD_SIZE)
        .astype(jnp.bfloat16)
    )
    mixed = jnp.dot(
        lax.all_gather(attended, "head", axis=1, tiled=True),
        out_weight,
        preferred_element_type=jnp.float32,
    )
    return mixed.astype(jnp.bfloat16)


def solution(mesh):
    in_specs = (P("ctx", "head"), P("ctx", "head"), P("ctx", "head"), P("ctx"), P(None, "head"))
    out_specs = P("ctx", "head")
    return jax.shard_map(shards, mesh=mesh, in_specs=in_specs, out_specs=out_specs, check_vma=False)
```

profile of v0, /device:TPU:1, one launch (start us, length us, event | category | flops | bytes accessed | tf_op | source)
XLA Modules:
  0.0 138.5 jit_solution(5916004114600088739)
XLA Ops:
  6.5 1.2 copy.18
  7.7 0.1 fusion.58
  7.8 0.2 copy.54
  8.0 0.2 copy.55
  8.2 0.8 fusion.40
  9.0 1.6 %multiply_cosine_fusion = (f32[512,64]{1,0:T(8,128)S(1)}, f32[512,64]{1,0:T(8,128)S(1)}) fusion(f32[64]{0:T(128)} %constant.404.clone, f32[512]{0:T(512)S(1)} %get-tuple-element.249), kind=kLoop, calls=%fused_computation.50 | loop fusion | flops 32768 | bytes 264448 | tf_op jit(solution)/shard_map/cos | solution.py:23
  10.6 0.1 multiply_subtract_fusion
  10.8 0.1 maximum_convert_fusion
  10.9 0.1 copy.25
  11.1 2.8 %collective-permute-start = (bf16[512,256]{0,1:T(8,128)(2,1)S(1)}, bf16[512,256]{0,1:T(8,128)(2,1)}, u32[]{:S(2)}, u32[]{:S(2)}) collective-permute-start(bf16[512,256]{0,1:T(8,128)(2,1)S(1)} %bitcast.211), channel_id=1, source_target_pairs={{0,2},{2,4},{4,6},{6,8},{8,10},{10,12},{12,14},{14,16},{16,18},{18... | collective-permute-start | bytes 786440 | tf_op jit(solution)/shard_map/ppermute | solution.py:16
  13.8 0.1 collective-permute-start.1
  13.9 1.1 copy.47
  15.1 0.2 convert_bitcast_fusion
  15.3 0.5 copy.58
  15.8 0.7 fusion.57
  16.5 0.8 subtract_convert_fusion
  17.3 0.6 pad_maximum_fusion
  17.9 1.0 compare_and_fusion.3
  18.9 4.7 %fusion = (f32[2,4,512]{2,1,0:T(4,128)S(1)}, f32[2,512,512,4]{2,1,3,0:T(8,128)}) fusion(pred[512,512]{0,1:T(8,128)(4,1)S(1)} %get-tuple-element.242, bf16[512,2,4,128]{3,0,2,1:T(8,128)(2,1)S(1)} %bitcast.202, bf16[512,2,128]{2,0,1:T(8,128)(2,1)S(1)} %maximum_convert_fusion), kind=kOutput, calls=%fused_computation.8 | convolution fusion | flops 543158272 | bytes 9977856 | tf_op jit(solution)/shard_map/qhgd,khd->hgqk/dot_general | solution.py:52
  23.6 0.0 collective-permute-done.1
  23.6 0.9 copy.27
  24.5 1.6 %collective-permute-start.3 = (bf16[512,256]{1,0:T(8,128)(2,1)S(1)}, bf16[512,256]{1,0:T(8,128)(2,1)S(1)}, u32[]{:S(2)}, u32[]{:S(2)}) collective-permute-start(bf16[512,256]{1,0:T(8,128)(2,1)S(1)} %collective-permute-done.1), channel_id=1, source_target_pairs={{0,2},{2,4},{4,6},{6,8},{8,10},{10,12},{12,14},{14,16},{16,18},{18... | collective-permute-start | bytes 786440 | tf_op jit(solution)/shard_map/ppermute | solution.py:16
  26.1 0.1 collective-permute-start.2
  26.2 5.9 %fusion.1 = (f32[2,4,512]{2,1,0:T(4,128)S(1)}, f32[2,512,512,4]{2,1,3,0:T(8,128)}) fusion(pred[512,512]{0,1:T(8,128)(4,1)S(1)} %get-tuple-element.243, bf16[512,2,128,1]{0,2,3,1:T(8,128)(2,1)} %bitcast.45, bf16[512,2,4,128]{3,0,2,1:T(8,128)(2,1)S(1)} %bitcast.203), kind=kOutput, calls=%fused_computation.9 | convolution fusion | flops 543158272 | bytes 9977856 | tf_op jit(solution)/shard_map/qhgd,khd->hgqk/dot_general | solution.py:52
  32.0 0.0 collective-permute-done.3
  32.1 0.8 copy.30
  32.9 1.2 collective-permute-start.5
  34.1 0.0 collective-permute-done.2
  34.1 0.5 collective-permute-start.4
  34.7 2.0 %fusion.2 = (f32[2,4,512]{2,1,0:T(4,128)S(1)}, f32[2,512,512,4]{2,1,3,0:T(8,128)S(1)}) fusion(pred[512,512]{0,1:T(8,128)(4,1)S(1)} %get-tuple-element.244, bf16[512,2,128,1]{0,2,3,1:T(8,128)(2,1)S(1)} %bitcast.209, bf16[512,2,4,128]{3,0,2,1:T(8,128)(2,1)S(1)} %bitcast.204), kind=kOutput, calls=%fused_computation.10 | convolution fusion | flops 543158272 | bytes 9977856 | tf_op jit(solution)/shard_map/qhgd,khd->hgqk/dot_general | solution.py:52
  36.7 6.2 %collective-permute-done.4 = bf16[512,256]{0,1:T(8,128)(2,1)S(1)} collective-permute-done((bf16[512,256]{0,1:T(8,128)(2,1)S(1)}, bf16[512,256]{0,1:T(8,128)(2,1)S(1)}, u32[]{:S(2)}, u32[]{:S(2)}) %collective-permute-start.4) | collective-permute-done | bytes 262176 | tf_op jit(solution)/shard_map/ppermute | solution.py:16
  42.9 2.0 %fusion.3 = (f32[2,4,512]{2,1,0:T(4,128)S(1)}, f32[2,512,512,4]{2,1,3,0:T(8,128)S(1)}) fusion(pred[512,512]{0,1:T(8,128)(4,1)S(1)} %get-tuple-element.245, bf16[512,2,128,1]{0,2,3,1:T(8,128)(2,1)S(1)} %bitcast.210, bf16[512,2,4,128]{3,0,2,1:T(8,128)(2,1)S(1)} %bitcast.205), kind=kOutput, calls=%fused_computation.11 | convolution fusion | flops 543158272 | bytes 9977856 | tf_op jit(solution)/shard_map/qhgd,khd->hgqk/dot_general | solution.py:52
  45.0 0.1 slice-done.1
  45.1 2.0 %fusion.4 = f32[2,4,512]{2,1,0:T(4,128)S(1)} fusion(f32[2,512,512,4]{2,1,3,0:T(8,128)S(1)} %bitcast.199, f32[2,4,512]{2,1,0:T(4,128)S(1)} %get-tuple-element.241, pred[512,512]{0,1:T(8,128)(4,1)S(1)} %get-tuple-element.242), kind=kLoop, calls=%fused_computation.12 | loop fusion | flops 10481664 | bytes 8683520 | tf_op jit(solution)/shard_map/reduce_sum | solution.py:62
  47.1 0.0 slice-start.3
  47.1 3.8 %fusion.18 = f32[2,4,512,128]{2,3,1,0:T(8,128)} fusion(bf16[512,2,128,1]{0,2,3,1:T(8,128)(2,1)S(1)} %bitcast.212, f32[2,512,512,4]{2,1,3,0:T(8,128)S(1)} %bitcast.199, f32[2,4,512]{2,1,0:T(4,128)S(1)} %get-tuple-element.241, pred[512,512]{0,1:T(8,128)(4,1)S(1)} %get-tuple-element.242), kind=kOutput, calls=%fused_computation.23 | convolution fusion | flops 547356672 | bytes 11026432 | tf_op jit(solution)/shard_map/hgqk,khd->qhgd/dot_general | solution.py:63
  51.0 1.0 slice-done.3
  52.0 2.0 %fusion.6 = f32[2,4,512]{2,1,0:T(4,128)S(1)} fusion(f32[2,512,512,4]{2,1,3,0:T(8,128)S(1)} %bitcast.201, f32[2,4,512]{2,1,0:T(4,128)S(1)} %get-tuple-element.230, pred[512,512]{0,1:T(8,128)(4,1)S(1)} %get-tuple-element.243), kind=kLoop, calls=%fused_computation.14 | loop fusion | flops 10481664 | bytes 8683520 | tf_op jit(solution)/shard_map/reduce_sum | solution.py:62
  54.0 3.9 %fusion.16 = f32[2,4,512,128]{2,3,1,0:T(8,128)} fusion(bf16[512,2,128,1]{0,2,3,1:T(8,128)(2,1)S(1)} %bitcast.213, f32[2,512,512,4]{2,1,3,0:T(8,128)S(1)} %bitcast.201, f32[2,4,512]{2,1,0:T(4,128)S(1)} %get-tuple-element.230, pred[512,512]{0,1:T(8,128)(4,1)S(1)} %get-tuple-element.243), kind=kOutput, calls=%fused_computation.22 | convolution fusion | flops 547356672 | bytes 11026432 | tf_op jit(solution)/shard_map/hgqk,khd->qhgd/dot_general | solution.py:63
  57.9 2.0 %fusion.8 = f32[2,4,512]{2,1,0:T(4,128)S(1)} fusion(f32[2,512,512,4]{2,1,3,0:T(8,128)S(1)} %get-tuple-element.253, f32[2,4,512]{2,1,0:T(4,128)S(1)} %get-tuple-element.229, pred[512,512]{0,1:T(8,128)(4,1)S(1)} %get-tuple-element.244), kind=kLoop, calls=%fused_computation.16 | loop fusion | flops 10481664 | bytes 8683520 | tf_op jit(solution)/shard_map/reduce_sum | solution.py:62
  59.9 3.8 %fusion.14 = f32[2,4,512,128]{2,3,1,0:T(8,128)} fusion(bf16[512,2,128,1]{0,2,3,1:T(8,128)(2,1)S(1)} %bitcast.214, f32[2,512,512,4]{2,1,3,0:T(8,128)S(1)} %get-tuple-element.253, f32[2,4,512]{2,1,0:T(4,128)S(1)} %get-tuple-element.229, pred[512,512]{0,1:T(8,128)(4,1)S(1)} %get-tuple-element.244), kind=kOutput, calls=%fused_computation.21 | convolution fusion | flops 547356672 | bytes 11026432 | tf_op jit(solution)/shard_map/hgqk,khd->qhgd/dot_general | solution.py:63
  63.7 2.0 %fusion.10 = f32[2,4,512]{2,1,0:T(4,128)S(1)} fusion(f32[2,512,512,4]{2,1,3,0:T(8,128)S(1)} %get-tuple-element.251, f32[2,4,512]{2,1,0:T(4,128)S(1)} %get-tuple-element.228, pred[512,512]{0,1:T(8,128)(4,1)S(1)} %get-tuple-element.245), kind=kLoop, calls=%fused_computation.18 | loop fusion | flops 10481664 | bytes 8683520 | tf_op jit(solution)/shard_map/reduce_sum | solution.py:62
  65.8 0.0 collective-permute-done.5
  65.8 0.1 copy.33
  66.0 9.1 %fusion.25 = bf16[512,2,4,128]{0,3,2,1:T(8,128)(2,1)} fusion(f32[2,4,512,128]{2,3,1,0:T(8,128)} %fusion.14, f32[2,4,512,128]{2,3,1,0:T(8,128)} %fusion.16, f32[2,4,512,128]{2,3,1,0:T(8,128)} %fusion.18, bf16[512,2,128,1]{0,2,3,1:T(8,128)(2,1)S(1)} %bitcast.215, f32[2,512,512,4]{2,1,3,0:T(8,128)} %copy-done, f32[2,4,512]{2,1,0:T(4,128)S(1)} %get-tuple-element.228, ...), kind=kOutput, calls=%fused_computation.31 | convolution fusion | flops 552075264 | bytes 16351232 | tf_op jit(solution)/shard_map/hgqk,khd->qhgd/dot_general | solution.py:63
  75.1 0.0 all-gather.2.cloned.1.call-update
  75.1 46.6 %all-gather.2.cloned.1.call-done = bf16[512,2048]{0,1:T(8,128)(2,1)} async-done(((bf16[512,1024]{0,1:T(8,128)(2,1)}), bf16[512,2048]{0,1:T(8,128)(2,1)}) %all-gather.2.cloned.1.call-update) | async-done | bytes 2097168 | tf_op jit(solution)/shard_map/all_gather | solution.py:131
  121.7 9.9 %convolution_convert_fusion = bf16[512,2048]{1,0:T(8,128)(2,1)} fusion(bf16[512,2048]{0,1:T(8,128)(2,1)} %all-gather.2.cloned.1.call-done, bf16[2048,2048]{1,0:T(8,128)(2,1)} %param.55), kind=kOutput, calls=%fused_computation.28 | convolution fusion | flops 4296015872 | bytes 12582912 | tf_op jit(solution)/shard_map/dot_general | solution.py:130
  (21 shorter events, 0.1 us)
Async XLA Ops:
  6.5 8.5 %copy-start.1 = (bf16[512,1024]{1,0:T(8,128)(2,1)S(1)}, bf16[512,1024]{1,0:T(8,128)(2,1)}, u32[]{:S(2)}) copy-start(bf16[512,1024]{1,0:T(8,128)(2,1)} %param.51) | copy-start | bytes 3145732
  6.5 115.2 %all-gather.2.cloned.1.call-start = ((), (), s32[]{:S(2)}) async-start(), calls=%async_computation | async-start | bytes 3145728 | tf_op jit(solution)/shard_map/all_gather | solution.py:131
  11.1 15.0 %collective-permute-start = (bf16[512,256]{0,1:T(8,128)(2,1)S(1)}, bf16[512,256]{0,1:T(8,128)(2,1)}, u32[]{:S(2)}, u32[]{:S(2)}) collective-permute-start(bf16[512,256]{0,1:T(8,128)(2,1)S(1)} %bitcast.211), channel_id=1, source_target_pairs={{0,2},{2,4},{4,6},{6,8},{8,10},{10,12},{12,14},{14,16},{16,18},{18... | collective-permute-start | bytes 786440 | tf_op jit(solution)/shard_map/ppermute | solution.py:16
  13.8 9.8 %collective-permute-start.1 = (bf16[512,256]{1,0:T(8,128)(2,1)}, bf16[512,256]{1,0:T(8,128)(2,1)S(1)}, u32[]{:S(2)}, u32[]{:S(2)}) collective-permute-start(bf16[512,256]{1,0:T(8,128)(2,1)} %param.53), channel_id=1, source_target_pairs={{0,2},{2,4},{4,6},{6,8},{8,10},{10,12},{12,14},{14,16},{16,18},{18... | collective-permute-start | bytes 786440 | tf_op jit(solution)/shard_map/ppermute | solution.py:16
  24.5 7.6 %collective-permute-start.3 = (bf16[512,256]{1,0:T(8,128)(2,1)S(1)}, bf16[512,256]{1,0:T(8,128)(2,1)S(1)}, u32[]{:S(2)}, u32[]{:S(2)}) collective-permute-start(bf16[512,256]{1,0:T(8,128)(2,1)S(1)} %collective-permute-done.1), channel_id=1, source_target_pairs={{0,2},{2,4},{4,6},{6,8},{8,10},{10,12},{12,14},{14,16},{16,18},{18... | collective-permute-start | bytes 786440 | tf_op jit(solution)/shard_map/ppermute | solution.py:16
  26.1 8.1 %collective-permute-start.2 = (bf16[512,256]{0,1:T(8,128)(2,1)}, bf16[512,256]{0,1:T(8,128)(2,1)S(1)}, u32[]{:S(2)}, u32[]{:S(2)}) collective-permute-start(bf16[512,256]{0,1:T(8,128)(2,1)} %collective-permute-done), channel_id=1, source_target_pairs={{0,2},{2,4},{4,6},{6,8},{8,10},{10,12},{12,14},{14,16},{16,18},{18... | collective-permute-start | bytes 786440 | tf_op jit(solution)/shard_map/ppermute | solution.py:16
  32.9 32.9 %collective-permute-start.5 = (bf16[512,256]{1,0:T(8,128)(2,1)S(1)}, bf16[512,256]{1,0:T(8,128)(2,1)S(1)}, u32[]{:S(2)}, u32[]{:S(2)}) collective-permute-start(bf16[512,256]{1,0:T(8,128)(2,1)S(1)} %collective-permute-done.3), channel_id=1, source_target_pairs={{0,2},{2,4},{4,6},{6,8},{8,10},{10,12},{12,14},{14,16},{16,18},{18... | collective-permute-start | bytes 786440 | tf_op jit(solution)/shard_map/ppermute | solution.py:16
  34.1 8.8 %collective-permute-start.4 = (bf16[512,256]{0,1:T(8,128)(2,1)S(1)}, bf16[512,256]{0,1:T(8,128)(2,1)S(1)}, u32[]{:S(2)}, u32[]{:S(2)}) collective-permute-start(bf16[512,256]{0,1:T(8,128)(2,1)S(1)} %collective-permute-done.2), channel_id=1, source_target_pairs={{0,2},{2,4},{4,6},{6,8},{8,10},{10,12},{12,14},{14,16},{16,18},{18... | collective-permute-start | bytes 786440 | tf_op jit(solution)/shard_map/ppermute | solution.py:16
  34.7 10.3 %slice-start = ((s8[8388608]{0:T(1024)(128)(4,1)}), s8[4194304]{0:T(1024)(128)(4,1)S(1)}, s32[]{:S(2)}) async-start(s8[8388608]{0:T(1024)(128)(4,1)} %bitcast.198), calls=%async_computation.1 | async-start | bytes 8388608
  42.9 2.2 %slice-start.1 = ((s8[8388608]{0:T(1024)(128)(4,1)}), s8[4194304]{0:T(1024)(128)(4,1)S(1)}, s32[]{:S(2)}) async-start(s8[8388608]{0:T(1024)(128)(4,1)} %bitcast.198), calls=%async_computation.2 | async-start | bytes 8388608
  44.9 18.8 %copy-start = (f32[2,512,512,4]{2,1,3,0:T(8,128)}, f32[2,512,512,4]{2,1,3,0:T(8,128)S(1)}, u32[]{:S(2)}) copy-start(f32[2,512,512,4]{2,1,3,0:T(8,128)S(1)} %get-tuple-element.251) | copy-start | bytes 25165828
  47.1 3.8 %slice-start.2 = ((s8[8388608]{0:T(1024)(128)(4,1)}), s8[4194304]{0:T(1024)(128)(4,1)S(1)}, s32[]{:S(2)}) async-start(s8[8388608]{0:T(1024)(128)(4,1)} %bitcast.200), calls=%async_computation.3 | async-start | bytes 8388608
  47.1 4.9 %slice-start.3 = ((s8[8388608]{0:T(1024)(128)(4,1)}), s8[4194304]{0:T(1024)(128)(4,1)S(1)}, s32[]{:S(2)}) async-start(s8[8388608]{0:T(1024)(128)(4,1)} %bitcast.200), calls=%async_computation.4 | async-start | bytes 8388608
  51.0 3.1 %copy-start.2 = (bf16[512,256]{0,1:T(8,128)(2,1)S(1)}, bf16[512,256]{0,1:T(8,128)(2,1)}, u32[]{:S(2)}) copy-start(bf16[512,256]{0,1:T(8,128)(2,1)} %copy.27) | copy-start | bytes 786436
  57.9 2.0 %copy-start.3 = (bf16[512,256]{0,1:T(8,128)(2,1)S(1)}, bf16[512,256]{0,1:T(8,128)(2,1)}, u32[]{:S(2)}) copy-start(bf16[512,256]{0,1:T(8,128)(2,1)} %copy.30) | copy-start | bytes 786436
Sparse Core Ops, SparseCore 0:
  75.2 46.4 all-gather.1
where the time goes:
time: 139 us; the launch traced here: 138 us
  waiting for transfers between devices  52.9 us (38%)
  matrix products  45.1 us (32%)
  between operations  13.7 us (10%)
  other arithmetic  13.5 us (10%)
  local copies, waits for them, and re-layouts  7.03 us (5%)
  starting transfers between devices  6.31 us (5%)
    all_gather x1, waiting for transfers between devices, shards(): lax.all_gather(attended, 'head', axis=1, tiled=True)  46.6 us
    dot_general x4, matrix products, attend(): jnp.einsum('hgqk,khd->qhgd', weights.astype(jnp.bfloat16), shaped_value,...  20.6 us
    dot_general x4, matrix products, attend(): jnp.einsum('qhgd,khd->hgqk', shaped_query, shaped_key, preferred_element_...  14.6 us
    dot_general x1, matrix products, shards(): jnp.dot(lax.all_gather(attended, 'head', axis=1, tiled=True), out_weight,...  9.9 us
    reduce_sum x4, other arithmetic, attend(): totals = totals * factor + jnp.sum(weights, axis=3)  8.1 us
    ppermute x6, starting transfers between devices, passed_along(): return lax.ppermute(value, axis, pairs)  6.31 us
    ppermute x6, waiting for transfers between devices, passed_along(): return lax.ppermute(value, axis, pairs)  6.22 us
    unnamed x20, local copies, waits for them, and re-layouts  3.2 us
  transfers between devices with their start and end apart: 7, of which 2 were waited for; matrix products, arithmetic and copies ran while one was open for 30% of the time, Pallas kernels for 0%

commit v1 on v0

--- a/solution.py
+++ b/solution.py
@@ -128,7 +128,10 @@
         .astype(jnp.bfloat16)
     )
     mixed = jnp.dot(
-        lax.all_gather(attended, "head", axis=1, tiled=True),
+        jnp.concatenate(
+            lax.all_to_all(jnp.stack([attended for _ in range(lax.psum(1, "head"))]), "head", 0, 0),
+            axis=1,
+        ),
         out_weight,
         preferred_element_type=jnp.float32,
     )

time: 139 us -> 108 us (0.78)
  the two profiles are of different devices: /device:TPU:1 before, /device:TPU:123 now
where the time goes in v1:
time: 108 us
  matrix products  43.3 us (40%)
  blocking collectives  29.3 us (27%)
  other arithmetic  13.7 us (13%)
  starting transfers between devices  12.3 us (11%)
  local copies, waits for them, and re-layouts  7.02 us (6%)
  waiting for transfers between devices  2.14 us (2%)
    all_to_all x1, blocking collectives, shards(): lax.all_to_all(jnp.stack([attended for _ in range(lax.psum(1, 'head'))]),...  29.3 us
    dot_general x4, matrix products, attend(): jnp.einsum('hgqk,khd->qhgd', weights.astype(jnp.bfloat16), shaped_value,...  19.6 us
    dot_general x4, matrix products, attend(): jnp.einsum('qhgd,khd->hgqk', shaped_query, shaped_key, preferred_element_...  14.6 us
    ppermute x6, starting transfers between devices, passed_along(): return lax.ppermute(value, axis, pairs)  12.3 us
    dot_general x1, matrix products, shards(): jnp.dot(jnp.concatenate(lax.all_to_all(jnp.stack([attended for _ in range...  9.1 us
    reduce_sum x4, other arithmetic, attend(): totals = totals * factor + jnp.sum(weights, axis=3)  8.1 us
    unnamed x20, local copies, waits for them, and re-layouts  3.19 us
  transfers between devices with their start and end apart: 6, of which 1 were waited for; matrix products, arithmetic and copies ran while one was open for 38% of the time, Pallas kernels for 0%

profile of v1, /device:TPU:123, one launch (start us, length us, event | category | flops | bytes accessed | tf_op | source)
XLA Modules:
  0.0 108.1 jit_solution(17598973808371512161)
XLA Ops:
  0.0 1.2 %copy.18 = bf16[512,256]{0,1:T(8,128)(2,1)S(1)} copy(bf16[512,256]{1,0:T(8,128)(2,1)} %param.52) | data formatting | bytes 524288 | tf_op args[1]
  1.2 0.1 fusion.58
  1.2 0.2 copy.54
  1.4 0.2 copy.55
  1.7 0.8 fusion.40
  2.4 1.6 %multiply_cosine_fusion = (f32[512,64]{1,0:T(8,128)S(1)}, f32[512,64]{1,0:T(8,128)S(1)}) fusion(f32[64]{0:T(128)} %constant.404.clone, f32[512]{0:T(512)S(1)} %get-tuple-element.249), kind=kLoop, calls=%fused_computation.51 | loop fusion | flops 32768 | bytes 264448 | tf_op jit(solution)/shard_map/cos | solution.py:23
  4.1 0.1 multiply_subtract_fusion
  4.2 0.1 maximum_convert_fusion
  4.4 0.1 copy.25
  4.5 3.1 %collective-permute-start = (bf16[512,256]{0,1:T(8,128)(2,1)S(1)}, bf16[512,256]{0,1:T(8,128)(2,1)}, u32[]{:S(2)}, u32[]{:S(2)}) collective-permute-start(bf16[512,256]{0,1:T(8,128)(2,1)S(1)} %bitcast.215), channel_id=1, source_target_pairs={{0,2},{2,4},{4,6},{6,8},{8,10},{10,12},{12,14},{14,16},{16,18},{18... | collective-permute-start | bytes 786440 | tf_op jit(solution)/shard_map/ppermute | solution.py:16
  7.6 0.1 collective-permute-start.1
  7.7 1.1 %copy.47 = bf16[512,256]{0,1:T(8,128)(2,1)S(1)} copy(bf16[512,256]{1,0:T(8,128)(2,1)} %param.53) | data formatting | bytes 524288 | tf_op jit(solution)/shard_map/reshape | solution.py:51
  8.9 0.2 convert_bitcast_fusion
  9.1 0.5 copy.58
  9.6 0.7 fusion.57
  10.3 0.8 subtract_convert_fusion
  11.1 0.6 pad_maximum_fusion.1
  11.7 1.0 compare_and_fusion.3
  12.8 4.7 %fusion = (f32[2,4,512]{2,1,0:T(4,128)S(1)}, f32[2,512,512,4]{2,1,3,0:T(8,128)}) fusion(pred[512,512]{0,1:T(8,128)(4,1)S(1)} %get-tuple-element.242, bf16[512,2,4,128]{3,0,2,1:T(8,128)(2,1)S(1)} %bitcast.205, bf16[512,2,128]{2,0,1:T(8,128)(2,1)S(1)} %maximum_convert_fusion), kind=kOutput, calls=%fused_computation.8 | convolution fusion | flops 543158272 | bytes 9977856 | tf_op jit(solution)/shard_map/qhgd,khd->hgqk/dot_general | solution.py:52
  17.5 0.0 collective-permute-done.1
  17.5 0.9 copy.27
  18.3 3.0 %collective-permute-start.3 = (bf16[512,256]{1,0:T(8,128)(2,1)S(1)}, bf16[512,256]{1,0:T(8,128)(2,1)S(1)}, u32[]{:S(2)}, u32[]{:S(2)}) collective-permute-start(bf16[512,256]{1,0:T(8,128)(2,1)S(1)} %collective-permute-done.1), channel_id=1, source_target_pairs={{0,2},{2,4},{4,6},{6,8},{8,10},{10,12},{12,14},{14,16},{16,18},{18... | collective-permute-start | bytes 786440 | tf_op jit(solution)/shard_map/ppermute | solution.py:16
  21.3 0.0 collective-permute-done
  21.3 0.0 collective-permute-start.2
  21.4 5.8 %fusion.1 = (f32[2,4,512]{2,1,0:T(4,128)S(1)}, f32[2,512,512,4]{2,1,3,0:T(8,128)}) fusion(pred[512,512]{0,1:T(8,128)(4,1)S(1)} %get-tuple-element.243, bf16[512,2,128,1]{0,2,3,1:T(8,128)(2,1)} %bitcast.47, bf16[512,2,4,128]{3,0,2,1:T(8,128)(2,1)S(1)} %bitcast.206), kind=kOutput, calls=%fused_computation.9 | convolution fusion | flops 543158272 | bytes 9977856 | tf_op jit(solution)/shard_map/qhgd,khd->hgqk/dot_general | solution.py:52
  27.2 0.0 collective-permute-done.3
  27.2 0.8 copy.30
  28.1 4.1 %collective-permute-start.5 = (bf16[512,256]{1,0:T(8,128)(2,1)S(1)}, bf16[512,256]{1,0:T(8,128)(2,1)S(1)}, u32[]{:S(2)}, u32[]{:S(2)}) collective-permute-start(bf16[512,256]{1,0:T(8,128)(2,1)S(1)} %collective-permute-done.3), channel_id=1, source_target_pairs={{0,2},{2,4},{4,6},{6,8},{8,10},{10,12},{12,14},{14,16},{16,18},{18... | collective-permute-start | bytes 786440 | tf_op jit(solution)/shard_map/ppermute | solution.py:16
  32.2 0.0 collective-permute-done.2
  32.2 2.0 %collective-permute-start.4 = (bf16[512,256]{0,1:T(8,128)(2,1)S(1)}, bf16[512,256]{0,1:T(8,128)(2,1)S(1)}, u32[]{:S(2)}, u32[]{:S(2)}) collective-permute-start(bf16[512,256]{0,1:T(8,128)(2,1)S(1)} %collective-permute-done.2), channel_id=1, source_target_pairs={{0,2},{2,4},{4,6},{6,8},{8,10},{10,12},{12,14},{14,16},{16,18},{18... | collective-permute-start | bytes 786440 | tf_op jit(solution)/shard_map/ppermute | solution.py:16
  34.2 2.0 %fusion.2 = (f32[2,4,512]{2,1,0:T(4,128)S(1)}, f32[2,512,512,4]{2,1,3,0:T(8,128)S(1)}) fusion(pred[512,512]{0,1:T(8,128)(4,1)S(1)} %get-tuple-element.244, bf16[512,2,128,1]{0,2,3,1:T(8,128)(2,1)S(1)} %bitcast.213, bf16[512,2,4,128]{3,0,2,1:T(8,128)(2,1)S(1)} %bitcast.207), kind=kOutput, calls=%fused_computation.10 | convolution fusion | flops 543158272 | bytes 9977856 | tf_op jit(solution)/shard_map/qhgd,khd->hgqk/dot_general | solution.py:52
  36.2 2.1 %collective-permute-done.4 = bf16[512,256]{0,1:T(8,128)(2,1)S(1)} collective-permute-done((bf16[512,256]{0,1:T(8,128)(2,1)S(1)}, bf16[512,256]{0,1:T(8,128)(2,1)S(1)}, u32[]{:S(2)}, u32[]{:S(2)}) %collective-permute-start.4) | collective-permute-done | bytes 262176 | tf_op jit(solution)/shard_map/ppermute | solution.py:16
  38.3 2.0 %fusion.3 = (f32[2,4,512]{2,1,0:T(4,128)S(1)}, f32[2,512,512,4]{2,1,3,0:T(8,128)S(1)}) fusion(pred[512,512]{0,1:T(8,128)(4,1)S(1)} %get-tuple-element.245, bf16[512,2,128,1]{0,2,3,1:T(8,128)(2,1)S(1)} %bitcast.214, bf16[512,2,4,128]{3,0,2,1:T(8,128)(2,1)S(1)} %bitcast.208), kind=kOutput, calls=%fused_computation.11 | convolution fusion | flops 543158272 | bytes 9977856 | tf_op jit(solution)/shard_map/qhgd,khd->hgqk/dot_general | solution.py:52
  40.4 0.1 slice-done.1
  40.5 2.0 %fusion.4 = f32[2,4,512]{2,1,0:T(4,128)S(1)} fusion(f32[2,512,512,4]{2,1,3,0:T(8,128)S(1)} %bitcast.202, f32[2,4,512]{2,1,0:T(4,128)S(1)} %get-tuple-element.241, pred[512,512]{0,1:T(8,128)(4,1)S(1)} %get-tuple-element.242), kind=kLoop, calls=%fused_computation.12 | loop fusion | flops 10481664 | bytes 8683520 | tf_op jit(solution)/shard_map/reduce_sum | solution.py:62
  42.6 0.0 slice-start.3
  42.6 3.8 %fusion.18 = f32[2,4,512,128]{2,3,1,0:T(8,128)} fusion(bf16[512,2,128,1]{0,2,3,1:T(8,128)(2,1)S(1)} %bitcast.216, f32[2,512,512,4]{2,1,3,0:T(8,128)S(1)} %bitcast.202, f32[2,4,512]{2,1,0:T(4,128)S(1)} %get-tuple-element.241, pred[512,512]{0,1:T(8,128)(4,1)S(1)} %get-tuple-element.242), kind=kOutput, calls=%fused_computation.23 | convolution fusion | flops 547356672 | bytes 11026432 | tf_op jit(solution)/shard_map/hgqk,khd->qhgd/dot_general | solution.py:63
  46.4 1.0 slice-done.3
  47.4 2.0 %fusion.6 = f32[2,4,512]{2,1,0:T(4,128)S(1)} fusion(f32[2,512,512,4]{2,1,3,0:T(8,128)S(1)} %bitcast.204, f32[2,4,512]{2,1,0:T(4,128)S(1)} %get-tuple-element.230, pred[512,512]{0,1:T(8,128)(4,1)S(1)} %get-tuple-element.243), kind=kLoop, calls=%fused_computation.14 | loop fusion | flops 10481664 | bytes 8683520 | tf_op jit(solution)/shard_map/reduce_sum | solution.py:62
  49.5 3.9 %fusion.16 = f32[2,4,512,128]{2,3,1,0:T(8,128)} fusion(bf16[512,2,128,1]{0,2,3,1:T(8,128)(2,1)S(1)} %bitcast.217, f32[2,512,512,4]{2,1,3,0:T(8,128)S(1)} %bitcast.204, f32[2,4,512]{2,1,0:T(4,128)S(1)} %get-tuple-element.230, pred[512,512]{0,1:T(8,128)(4,1)S(1)} %get-tuple-element.243), kind=kOutput, calls=%fused_computation.22 | convolution fusion | flops 547356672 | bytes 11026432 | tf_op jit(solution)/shard_map/hgqk,khd->qhgd/dot_general | solution.py:63
  53.3 2.0 %fusion.8 = f32[2,4,512]{2,1,0:T(4,128)S(1)} fusion(f32[2,512,512,4]{2,1,3,0:T(8,128)S(1)} %get-tuple-element.253, f32[2,4,512]{2,1,0:T(4,128)S(1)} %get-tuple-element.229, pred[512,512]{0,1:T(8,128)(4,1)S(1)} %get-tuple-element.244), kind=kLoop, calls=%fused_computation.16 | loop fusion | flops 10481664 | bytes 8683520 | tf_op jit(solution)/shard_map/reduce_sum | solution.py:62
  55.4 3.8 %fusion.14 = f32[2,4,512,128]{2,3,1,0:T(8,128)} fusion(bf16[512,2,128,1]{0,2,3,1:T(8,128)(2,1)S(1)} %bitcast.218, f32[2,512,512,4]{2,1,3,0:T(8,128)S(1)} %get-tuple-element.253, f32[2,4,512]{2,1,0:T(4,128)S(1)} %get-tuple-element.229, pred[512,512]{0,1:T(8,128)(4,1)S(1)} %get-tuple-element.244), kind=kOutput, calls=%fused_computation.21 | convolution fusion | flops 547356672 | bytes 11026432 | tf_op jit(solution)/shard_map/hgqk,khd->qhgd/dot_general | solution.py:63
  59.2 2.0 %fusion.10 = f32[2,4,512]{2,1,0:T(4,128)S(1)} fusion(f32[2,512,512,4]{2,1,3,0:T(8,128)S(1)} %get-tuple-element.251, f32[2,4,512]{2,1,0:T(4,128)S(1)} %get-tuple-element.228, pred[512,512]{0,1:T(8,128)(4,1)S(1)} %get-tuple-element.245), kind=kLoop, calls=%fused_computation.18 | loop fusion | flops 10481664 | bytes 8683520 | tf_op jit(solution)/shard_map/reduce_sum | solution.py:62
  61.3 0.1 copy.33
  61.4 8.1 %fusion.25 = bf16[512,2,4,128]{0,3,2,1:T(8,128)(2,1)S(1)} fusion(f32[2,4,512,128]{2,3,1,0:T(8,128)} %fusion.14, f32[2,4,512,128]{2,3,1,0:T(8,128)} %fusion.16, f32[2,4,512,128]{2,3,1,0:T(8,128)} %fusion.18, bf16[512,2,128,1]{0,2,3,1:T(8,128)(2,1)S(1)} %bitcast.219, f32[2,512,512,4]{2,1,3,0:T(8,128)} %copy-done, f32[2,4,512]{2,1,0:T(4,128)S(1)} %get-tuple-element.228, ...), kind=kOutput, calls=%fused_computation.32 | convolution fusion | flops 552075264 | bytes 16351232 | tf_op jit(solution)/shard_map/hgqk,khd->qhgd/dot_general | solution.py:63
  69.5 0.2 pad_maximum_fusion
  69.7 29.3 %all_to_all.5 = bf16[2,512,1024]{1,2,0:T(8,128)(2,1)S(1)} all-to-all(bf16[2,512,1024]{1,2,0:T(8,128)(2,1)S(1)} %pad_maximum_fusion), channel_id=1, replica_groups=mesh['ctx'=128,'head'=2] {'head'}, dimensions={0} | all-to-all | bytes 4194304 | tf_op jit(solution)/shard_map/all_to_all | solution.py:132
  99.0 9.1 %convolution_convert_fusion = bf16[512,2048]{1,0:T(8,128)(2,1)} fusion(bf16[512,2048]{0,1:T(8,128)(2,1)S(1)} %bitcast.211, bf16[2048,2048]{1,0:T(8,128)(2,1)} %param.55), kind=kOutput, calls=%fused_computation.28 | convolution fusion | flops 4296015872 | bytes 12582912 | tf_op jit(solution)/shard_map/dot_general | solution.py:130
  (20 shorter events, 0.1 us)
Async XLA Ops:
  0.0 8.9 %copy-start.1 = (bf16[512,1024]{1,0:T(8,128)(2,1)S(1)}, bf16[512,1024]{1,0:T(8,128)(2,1)}, u32[]{:S(2)}) copy-start(bf16[512,1024]{1,0:T(8,128)(2,1)} %param.51) | copy-start | bytes 3145732
  4.5 16.8 %collective-permute-start = (bf16[512,256]{0,1:T(8,128)(2,1)S(1)}, bf16[512,256]{0,1:T(8,128)(2,1)}, u32[]{:S(2)}, u32[]{:S(2)}) collective-permute-start(bf16[512,256]{0,1:T(8,128)(2,1)S(1)} %bitcast.215), channel_id=1, source_target_pairs={{0,2},{2,4},{4,6},{6,8},{8,10},{10,12},{12,14},{14,16},{16,18},{18... | collective-permute-start | bytes 786440 | tf_op jit(solution)/shard_map/ppermute | solution.py:16
  7.6 9.8 %collective-permute-start.1 = (bf16[512,256]{1,0:T(8,128)(2,1)}, bf16[512,256]{1,0:T(8,128)(2,1)S(1)}, u32[]{:S(2)}, u32[]{:S(2)}) collective-permute-start(bf16[512,256]{1,0:T(8,128)(2,1)} %param.53), channel_id=1, source_target_pairs={{0,2},{2,4},{4,6},{6,8},{8,10},{10,12},{12,14},{14,16},{16,18},{18... | collective-permute-start | bytes 786440 | tf_op jit(solution)/shard_map/ppermute | solution.py:16
  18.3 8.9 %collective-permute-start.3 = (bf16[512,256]{1,0:T(8,128)(2,1)S(1)}, bf16[512,256]{1,0:T(8,128)(2,1)S(1)}, u32[]{:S(2)}, u32[]{:S(2)}) collective-permute-start(bf16[512,256]{1,0:T(8,128)(2,1)S(1)} %collective-permute-done.1), channel_id=1, source_target_pairs={{0,2},{2,4},{4,6},{6,8},{8,10},{10,12},{12,14},{14,16},{16,18},{18... | collective-permute-start | bytes 786440 | tf_op jit(solution)/shard_map/ppermute | solution.py:16
  21.3 10.9 %collective-permute-start.2 = (bf16[512,256]{0,1:T(8,128)(2,1)}, bf16[512,256]{0,1:T(8,128)(2,1)S(1)}, u32[]{:S(2)}, u32[]{:S(2)}) collective-permute-start(bf16[512,256]{0,1:T(8,128)(2,1)} %collective-permute-done), channel_id=1, source_target_pairs={{0,2},{2,4},{4,6},{6,8},{8,10},{10,12},{12,14},{14,16},{16,18},{18... | collective-permute-start | bytes 786440 | tf_op jit(solution)/shard_map/ppermute | solution.py:16
  28.1 33.2 %collective-permute-start.5 = (bf16[512,256]{1,0:T(8,128)(2,1)S(1)}, bf16[512,256]{1,0:T(8,128)(2,1)S(1)}, u32[]{:S(2)}, u32[]{:S(2)}) collective-permute-start(bf16[512,256]{1,0:T(8,128)(2,1)S(1)} %collective-permute-done.3), channel_id=1, source_target_pairs={{0,2},{2,4},{4,6},{6,8},{8,10},{10,12},{12,14},{14,16},{16,18},{18... | collective-permute-start | bytes 786440 | tf_op jit(solution)/shard_map/ppermute | solution.py:16
  32.2 6.1 %collective-permute-start.4 = (bf16[512,256]{0,1:T(8,128)(2,1)S(1)}, bf16[512,256]{0,1:T(8,128)(2,1)S(1)}, u32[]{:S(2)}, u32[]{:S(2)}) collective-permute-start(bf16[512,256]{0,1:T(8,128)(2,1)S(1)} %collective-permute-done.2), channel_id=1, source_target_pairs={{0,2},{2,4},{4,6},{6,8},{8,10},{10,12},{12,14},{14,16},{16,18},{18... | collective-permute-start | bytes 786440 | tf_op jit(solution)/shard_map/ppermute | solution.py:16
  34.2 6.2 %slice-start = ((s8[8388608]{0:T(1024)(128)(4,1)}), s8[4194304]{0:T(1024)(128)(4,1)S(1)}, s32[]{:S(2)}) async-start(s8[8388608]{0:T(1024)(128)(4,1)} %bitcast.201), calls=%async_computation.1 | async-start | bytes 8388608
  38.3 2.2 %slice-start.1 = ((s8[8388608]{0:T(1024)(128)(4,1)}), s8[4194304]{0:T(1024)(128)(4,1)S(1)}, s32[]{:S(2)}) async-start(s8[8388608]{0:T(1024)(128)(4,1)} %bitcast.201), calls=%async_computation.2 | async-start | bytes 8388608
  40.4 18.8 %copy-start = (f32[2,512,512,4]{2,1,3,0:T(8,128)}, f32[2,512,512,4]{2,1,3,0:T(8,128)S(1)}, u32[]{:S(2)}) copy-start(f32[2,512,512,4]{2,1,3,0:T(8,128)S(1)} %get-tuple-element.251) | copy-start | bytes 25165828
  42.5 3.9 %slice-start.2 = ((s8[8388608]{0:T(1024)(128)(4,1)}), s8[4194304]{0:T(1024)(128)(4,1)S(1)}, s32[]{:S(2)}) async-start(s8[8388608]{0:T(1024)(128)(4,1)} %bitcast.203), calls=%async_computation.3 | async-start | bytes 8388608
  42.6 4.9 %slice-start.3 = ((s8[8388608]{0:T(1024)(128)(4,1)}), s8[4194304]{0:T(1024)(128)(4,1)S(1)}, s32[]{:S(2)}) async-start(s8[8388608]{0:T(1024)(128)(4,1)} %bitcast.203), calls=%async_computation.4 | async-start | bytes 8388608
  46.4 3.1 %copy-start.2 = (bf16[512,256]{0,1:T(8,128)(2,1)S(1)}, bf16[512,256]{0,1:T(8,128)(2,1)}, u32[]{:S(2)}) copy-start(bf16[512,256]{0,1:T(8,128)(2,1)} %copy.27) | copy-start | bytes 786436
  53.3 2.0 %copy-start.3 = (bf16[512,256]{0,1:T(8,128)(2,1)S(1)}, bf16[512,256]{0,1:T(8,128)(2,1)}, u32[]{:S(2)}) copy-start(bf16[512,256]{0,1:T(8,128)(2,1)} %copy.30) | copy-start | bytes 786436
